TPU v7x, 32 devices: a whole 2x2x4 slice. The times are simulated.
32 devices in a mesh: row: 4 (over z), col: 8 (over y, x, core).
Axes of the slice: x: 2, y: 2, z: 4, core: 2. Of those that a mesh axis runs over, the one named last changes fastest.
Arguments:
- rhs_front: float32 [4, 6144, 1024], P(None, 'row', 'col'), may hold values from -6 to 6
- lower_blocks: float32 [6, 6144, 6144], P(None, 'row', 'col'), may hold values from -0.046875 to 0.046875
- panel_inverse: float32 [4, 6144, 6144], P(None, 'col', 'row'), may hold values from -0.078125 to 0.078125
- child_rows: float32 [4, 64, 128, 1024], P('row', 'col'), may hold values from -4 to 4
- child_map: int32 [4, 64], P('row', 'col'), may hold values from 0 to 47
- child_owner: int32 [8, 24, 1], P('col'), may hold values from 0 to 3; in each aligned block of 24 rows (0 to 23, 24 to 47, ..., all dimensions but the last counted through in order) at most 7 rows name the same one
Outputs:
- solution: float32 [4, 6144, 1024], P(None, 'col')
- child_rhs: float32 [8, 4, 7, 128, 1024], P('col', 'row')
Inputs may be any that keep to these rules, and one draw needn't show every extreme that they name: `child_map`: several child update blocks may name the same front block. `child_owner`: of the 24 solved blocks of one column group, at most 7 name the same row group, and in some column group one row group is named exactly 7 times.
All inputs are finite; a program needn't handle non-finite values.
Results may differ from a plain program's by a relative error of at most 0.00012.
Values sent between devices are 32-bit elements; how exact they have to be, the bound alone decides.
A program may use at most 192 MiB of HBM per device.

v0:
```python
import jax
import jax.numpy as jnp
from jax import lax
from jax.sharding import PartitionSpec as P


def on_device(rhs_front, lower_blocks, panel_inverse, child_rows, child_map, child_owner):
    highest = lax.Precision.HIGHEST
    row_count = lax.axis_size("row")
    row_at = lax.axis_index("row")
    col_at = lax.axis_index("col")
    panels, row_span, narrow = rhs_front.shape
    col_span = panel_inverse.shape[1]
    block = child_rows.shape[2]
    width = child_rows.shape[3]
    local_blocks = panels * row_span // block
    per_panel = col_span // block
    held_blocks = panels * per_panel
    most = max(2, held_blocks // row_count + 1)
    share = width // row_count
    targets = jnp.arange(local_blocks, dtype=jnp.int32)
    picks = (child_map[0][None, :] == targets[:, None]).astype(jnp.float32)
    added = jnp.einsum("lk,kbr->lbr", picks, child_rows[0], precision=highest).reshape(
        panels, row_span, width
    )
    placed = lax.dynamic_update_slice(
        jnp.zeros((panels, row_span, width), jnp.float32), rhs_front, (0, 0, col_at * narrow)
    )
    assembled = added + placed
    owner = child_owner[0, :, 0]
    hits = (owner[None, :] == jnp.arange(row_count, dtype=jnp.int32)[:, None]).astype(jnp.int32)
    ranks = jnp.cumsum(hits, axis=1) - hits
    slot_match = (ranks[:, None, :] == jnp.arange(most, dtype=jnp.int32)[None, :, None]).astype(
        jnp.int32
    )
    routing = (hits[:, None, :] * slot_match).astype(jnp.float32)
    solved = []
    for panel in range(panels):
        front = assembled[panel]
        for prior in range(panel):
            front = front - jnp.dot(
                lower_blocks[panel * (panel - 1) // 2 + prior],
                solved[prior],
                precision=highest,
                preferred_element_type=jnp.float32,
            )
        front = lax.psum(front, "col")
        partial_value = jnp.dot(
            panel_inverse[panel], front, precision=highest, preferred_element_type=jnp.float32
        )
        current = lax.psum(partial_value, "row")
        solved.append(current)
    solution = jnp.stack(solved)
    mine = lax.dynamic_slice_in_dim(
        solution.reshape(held_blocks, block, width), row_at * share, share, 2
    )
    sending = jnp.einsum("dsk,kbr->dsbr", routing, mine, precision=highest)
    received = lax.all_to_all(sending, "row", split_axis=0, concat_axis=3, tiled=True)
    return (solution, received.reshape(1, 1, most, block, width))


def solution(mesh):
    return jax.shard_map(
        on_device,
        mesh=mesh,
        in_specs=(
            P(None, "row", "col"),
            P(None, "row", "col"),
            P(None, "col", "row"),
            P("row", "col", None, None),
            P("row", "col"),
            P("col", None, None),
        ),
        out_specs=(P(None, "col", None), P("col", "row", None, None, None)),
        check_vma=False,
    )
```

profile of v0, /device:TPU:0, one launch (start us, length us, event | category | flops | bytes accessed | tf_op | source)
XLA Modules:
  0.0 1298.2 jit_solution(18290730721862400627)
XLA Ops:
  7.2 16.1 %fusion.38 = f32[48,128,1024]{2,0,1:T(8,128)S(1)} fusion(f32[8,128,1024]{2,1,0:T(8,128)} %bitcast.124, s32[8]{0:T(128)} %bitcast.129), kind=kOutput, calls=%fused_computation.41 | convolution fusion | flops 603980160 | bytes 29360160 | tf_op jit(solution)/shard_map/lk,kbr->lbr/dot_general | solution.py:23
  23.3 27.6 %copy.18 = f32[48,128,1024]{2,1,0:T(8,128)} copy(f32[48,128,1024]{2,0,1:T(8,128)S(1)} %fusion.38) | data formatting | bytes 50331648 | tf_op jit(solution)/shard_map/lk,kbr->lbr/dot_general | solution.py:23
  50.9 25.1 %copy.21 = f32[4,1536,1024]{1,2,0:T(8,128)} copy(f32[4,1536,1024]{2,1,0:T(8,128)} %bitcast.120) | data formatting | bytes 50331648 | tf_op jit(solution)/shard_map/reshape | solution.py:23
  76.0 2.4 copy.20
  78.4 4.1 add_dynamic-update-slice_fusion
  82.5 5.9 slice_bitcast_fusion.3
  88.5 106.8 %all-reduce.9.cloned.1.call-done = f32[1536,1024]{0,1:T(8,128)} async-done(((f32[1536,1024]{0,1:T(8,128)}), f32[1536,1024]{0,1:T(8,128)}) %all-reduce.9.cloned.1.call-update) | async-done | bytes 6291472 | tf_op jit(solution)/shard_map/psum | solution.py:47
  195.3 19.5 %fusion.45 = f32[768,1024]{0,1:T(8,128)} fusion(f32[1536,1024]{0,1:T(8,128)} %all-reduce.9.cloned.1.call-done, f32[4,768,1536]{2,1,0:T(8,128)} %param.8), kind=kOutput, calls=%fused_computation.46 | convolution fusion | flops 14495514624 | bytes 14155776 | tf_op jit(solution)/shard_map/dot_general | solution.py:48
  214.9 121.3 %all-reduce.11.cloned.1.call-done = f32[768,1024]{0,1:T(8,128)} async-done(((f32[768,1024]{0,1:T(8,128)}), f32[768,1024]{0,1:T(8,128)}) %all-reduce.11.cloned.1.call-update) | async-done | bytes 3145744 | tf_op jit(solution)/shard_map/psum | solution.py:51
  336.1 19.6 %fusion.5 = f32[1536,1024]{0,1:T(8,128)} fusion(f32[4,1536,1024]{1,2,0:T(8,128)} %add_dynamic-update-slice_fusion, f32[768,1024]{0,1:T(8,128)} %all-reduce.11.cloned.1.call-done, f32[6,1536,768]{2,1,0:T(8,128)} %param.7), kind=kOutput, calls=%fused_computation.9 | convolution fusion | flops 14497087488 | bytes 20447232 | tf_op jit(solution)/shard_map/dot_general | solution.py:41
  355.8 103.0 %all-reduce.13.cloned.1.call-done = f32[1536,1024]{0,1:T(8,128)} async-done(((f32[1536,1024]{0,1:T(8,128)}), f32[1536,1024]{0,1:T(8,128)}) %all-reduce.13.cloned.1.call-update) | async-done | bytes 6291472 | tf_op jit(solution)/shard_map/psum | solution.py:47
  458.9 19.6 %fusion.48 = f32[768,1024]{0,1:T(8,128)} fusion(f32[1536,1024]{0,1:T(8,128)} %all-reduce.13.cloned.1.call-done, f32[4,768,1536]{2,1,0:T(8,128)} %param.8), kind=kOutput, calls=%fused_computation.47 | convolution fusion | flops 14495514624 | bytes 14155776 | tf_op jit(solution)/shard_map/dot_general | solution.py:48
  478.6 121.3 %all-reduce.15.cloned.1.call-done = f32[768,1024]{0,1:T(8,128)} async-done(((f32[768,1024]{0,1:T(8,128)}), f32[768,1024]{0,1:T(8,128)}) %all-reduce.15.cloned.1.call-update) | async-done | bytes 3145744 | tf_op jit(solution)/shard_map/psum | solution.py:51
  599.8 18.3 %fusion.16 = f32[1024,1536]{1,0:T(8,128)S(1)} fusion(f32[768,1024]{0,1:T(8,128)} %all-reduce.15.cloned.1.call-done, f32[6,1536,768]{2,1,0:T(8,128)} %param.7), kind=kOutput, calls=%fused_computation.21 | convolution fusion | flops 14495514624 | bytes 14155776 | tf_op jit(solution)/shard_map/dot_general | solution.py:41
  618.1 19.5 %fusion.4 = f32[1536,1024]{0,1:T(8,128)} fusion(f32[4,1536,1024]{1,2,0:T(8,128)} %add_dynamic-update-slice_fusion, f32[1024,1536]{1,0:T(8,128)S(1)} %fusion.16, f32[768,1024]{0,1:T(8,128)S(1)} %copy-done, f32[6,1536,768]{2,1,0:T(8,128)} %param.7), kind=kOutput, calls=%fused_computation.7 | convolution fusion | flops 14498660352 | bytes 26738688 | tf_op jit(solution)/shard_map/dot_general | solution.py:41
  637.7 103.0 %all-reduce.17.cloned.1.call-done = f32[1536,1024]{0,1:T(8,128)} async-done(((f32[1536,1024]{0,1:T(8,128)}), f32[1536,1024]{0,1:T(8,128)}) %all-reduce.17.cloned.1.call-update) | async-done | bytes 6291472 | tf_op jit(solution)/shard_map/psum | solution.py:47
  740.7 19.5 %fusion.51 = f32[768,1024]{0,1:T(8,128)} fusion(f32[1536,1024]{0,1:T(8,128)} %all-reduce.17.cloned.1.call-done, f32[4,768,1536]{2,1,0:T(8,128)} %param.8), kind=kOutput, calls=%fused_computation.48 | convolution fusion | flops 14495514624 | bytes 14155776 | tf_op jit(solution)/shard_map/dot_general | solution.py:48
  760.3 20.1 %fusion.10 = f32[1024,1536]{1,0:T(8,128)} fusion(f32[768,1024]{0,1:T(8,128)} %all-reduce.15.cloned.1.call-done, f32[6,1536,768]{2,1,0:T(8,128)} %param.7), kind=kOutput, calls=%fused_computation.15 | convolution fusion | flops 14495514624 | bytes 14155776 | tf_op jit(solution)/shard_map/dot_general | solution.py:41
  780.4 101.2 %all-reduce.19.cloned.1.call-done = f32[768,1024]{0,1:T(8,128)} async-done(((f32[768,1024]{0,1:T(8,128)}), f32[768,1024]{0,1:T(8,128)}) %all-reduce.19.cloned.1.call-update) | async-done | bytes 3145744 | tf_op jit(solution)/shard_map/psum | solution.py:51
  881.6 18.8 %fusion.8 = f32[1024,1536]{1,0:T(8,128)S(1)} fusion(f32[768,1024]{0,1:T(8,128)} %all-reduce.19.cloned.1.call-done, f32[6,1536,768]{2,1,0:T(8,128)} %param.7), kind=kOutput, calls=%fused_computation.13 | convolution fusion | flops 14495514624 | bytes 14155776 | tf_op jit(solution)/shard_map/dot_general | solution.py:41
  900.4 19.7 %fusion.2 = f32[1536,1024]{0,1:T(8,128)} fusion(f32[4,1536,1024]{1,2,0:T(8,128)} %add_dynamic-update-slice_fusion, f32[1024,1536]{1,0:T(8,128)S(1)} %fusion.8, f32[1024,1536]{1,0:T(8,128)S(1)} %copy-done.1, f32[768,1024]{0,1:T(8,128)S(1)} %copy-done, f32[6,1536,768]{2,1,0:T(8,128)} %param.7), kind=kOutput, calls=%fused_computation.4 | convolution fusion | flops 14500233216 | bytes 33030144 | tf_op jit(solution)/shard_map/dot_general | solution.py:41
  920.2 103.0 %all-reduce.21.cloned.1.call-done = f32[1536,1024]{0,1:T(8,128)} async-done(((f32[1536,1024]{0,1:T(8,128)}), f32[1536,1024]{0,1:T(8,128)}) %all-reduce.21.cloned.1.call-update) | async-done | bytes 6291472 | tf_op jit(solution)/shard_map/psum | solution.py:47
  1023.2 19.7 %fusion.54 = f32[1,768,1024]{1,2,0:T(8,128)} fusion(f32[1536,1024]{0,1:T(8,128)} %all-reduce.21.cloned.1.call-done, f32[4,768,1536]{2,1,0:T(8,128)} %param.8), kind=kOutput, calls=%fused_computation.49 | convolution fusion | flops 14495514624 | bytes 14155776 | tf_op jit(solution)/shard_map/dot_general | solution.py:48
  1043.1 121.1 %all-reduce.23.cloned.1.call-done = f32[1,768,1024]{1,2,0:T(8,128)} async-done(((f32[1,768,1024]{1,2,0:T(8,128)}), f32[1,768,1024]{1,2,0:T(8,128)}) %all-reduce.23.cloned.1.call-update) | async-done | bytes 3145744 | tf_op jit(solution)/shard_map/psum | solution.py:51
  1164.2 9.1 pad_maximum_fusion
  1173.3 12.6 copy.26
  1185.9 2.2 constant_dynamic-slice_fusion
  1188.1 6.7 fusion.44
  1194.8 1.1 copy.24
  1196.0 85.4 %all_to_all.15 = f32[4,7,128,256]{3,2,1,0:T(8,128)} all-to-all(f32[4,7,128,256]{3,2,1,0:T(8,128)S(1)} %copy.24), channel_id=1, replica_groups=mesh['row'=4,'col'=8] {'row'}, dimensions={0} | all-to-all | bytes 7340032 | tf_op jit(solution)/shard_map/all_to_all | solution.py:58
  1281.4 4.6 copy.25
  1286.0 5.0 copy.27
  (25 shorter events, 0.7 us)
Async XLA Ops:
  7.2 188.1 %all-reduce.9.cloned.1.call-start = ((), (), s32[]{:S(2)}) async-start(), calls=%async_computation.1 | async-start | bytes 12582912 | tf_op jit(solution)/shard_map/psum | solution.py:47
  88.4 247.7 %all-reduce.11.cloned.1.call-start = ((), (), s32[]{:S(2)}) async-start(), calls=%async_computation.2 | async-start | bytes 6291456 | tf_op jit(solution)/shard_map/psum | solution.py:51
  214.8 244.0 %all-reduce.13.cloned.1.call-start = ((), (), s32[]{:S(2)}) async-start(), calls=%async_computation.3 | async-start | bytes 12582912 | tf_op jit(solution)/shard_map/psum | solution.py:47
  355.8 244.1 %all-reduce.15.cloned.1.call-start = ((), (), s32[]{:S(2)}) async-start(), calls=%async_computation.4 | async-start | bytes 6291456 | tf_op jit(solution)/shard_map/psum | solution.py:51
  478.5 139.6 %copy-start = (f32[768,1024]{0,1:T(8,128)S(1)}, f32[768,1024]{0,1:T(8,128)}, u32[]{:S(2)}) copy-start(f32[768,1024]{0,1:T(8,128)} %all-reduce.11.cloned.1.call-done) | copy-start | bytes 9437188
  478.5 262.2 %all-reduce.17.cloned.1.call-start = ((), (), s32[]{:S(2)}) async-start(), calls=%async_computation.5 | async-start | bytes 12582912 | tf_op jit(solution)/shard_map/psum | solution.py:47
  637.7 243.9 %all-reduce.19.cloned.1.call-start = ((), (), s32[]{:S(2)}) async-start(), calls=%async_computation.6 | async-start | bytes 6291456 | tf_op jit(solution)/shard_map/psum | solution.py:51
  760.3 262.9 %all-reduce.21.cloned.1.call-start = ((), (), s32[]{:S(2)}) async-start(), calls=%async_computation.7 | async-start | bytes 12582912 | tf_op jit(solution)/shard_map/psum | solution.py:47
  881.6 18.8 %copy-start.1 = (f32[1024,1536]{1,0:T(8,128)S(1)}, f32[1024,1536]{1,0:T(8,128)}, u32[]{:S(2)}) copy-start(f32[1024,1536]{1,0:T(8,128)} %fusion.10) | copy-start | bytes 18874372
  920.1 122.8 %copy-start.2 = (s32[1,24,1]{1,2,0:T(1,128)S(1)}, s32[1,24,1]{1,2,0:T(1,128)}, u32[]{:S(2)}) copy-start(s32[1,24,1]{1,2,0:T(1,128)} %param.11) | copy-start | bytes 292
  920.1 244.1 %all-reduce.23.cloned.1.call-start = ((), (), s32[]{:S(2)}) async-start(), calls=%async_computation.8 | async-start | bytes 6291456 | tf_op jit(solution)/shard_map/psum | solution.py:51
Sparse Core Ops, SparseCore 0:
  88.6 106.6 all-reduce.8
  214.9 121.1 all-reduce.10
  355.9 102.9 all-reduce.12
  478.6 121.1 all-reduce.14
  637.8 102.9 all-reduce.16
  760.4 121.1 all-reduce.18
  920.2 102.8 all-reduce.20
  1043.0 121.1 all-reduce.22
where the time goes:
time: 1310 us; the launch traced here: 1300 us
  waiting for transfers between devices  881 us (67%)
  matrix products  217 us (17%)
  local copies, waits for them, and re-layouts  86.5 us (7%)
  blocking collectives  85.4 us (7%)
  between operations  14.6 us (1%)
  other arithmetic  13.4 us (1%)
    psum x4, waiting for transfers between devices, on_device(): current = lax.psum(partial_value, 'row')  465 us
    psum x4, waiting for transfers between devices, on_device(): front = lax.psum(front, 'col')  416 us
    dot_general x6, matrix products, on_device(): jnp.dot(lower_blocks[panel * (panel - 1) // 2 + prior], solved[prior], pr...  116 us
    all_to_all x1, blocking collectives, on_device(): lax.all_to_all(sending, 'row', split_axis=0, concat_axis=3, tiled=True)  85.4 us
    dot_general x4, matrix products, on_device(): jnp.dot(panel_inverse[panel], front, precision=highest, preferred_element...  78.3 us
    dot_general x1, local copies, waits for them, and re-layouts, on_device(): jnp.einsum('lk,kbr->lbr', picks, child_rows[0], precision=highest)  27.6 us
  transfers between devices with their start and end apart: 8, of which 8 were waited for; matrix products, arithmetic and copies ran while one was open for 2% of the time, Pallas kernels for 0%

commit v1 on v0

--- a/solution.py
+++ b/solution.py
@@ -2,6 +2,29 @@
 import jax.numpy as jnp
 from jax import lax
 from jax.sharding import PartitionSpec as P
+
+
+def in_blocks(array, dim, peers):
+    shape = array.shape
+    tiles = array.reshape(*shape[:dim], peers, shape[dim] // peers, *shape[dim + 1 :])
+    return jnp.moveaxis(tiles, dim, 0)
+
+
+def laid_out(blocks, dim):
+    dims = list(blocks.shape[1:])
+    dims[dim] *= blocks.shape[0]
+    return jnp.moveaxis(blocks, 0, dim).reshape(dims)
+
+
+def pairwise_exchange(shard, axis, split_dim, concat_dim):
+    size, here = (lax.axis_size(axis), lax.axis_index(axis))
+    blocks = in_blocks(shard, split_dim, size)
+    outs = [blocks[here]]
+    for step in range(1, size):
+        sent = blocks[here ^ step]
+        outs.append(lax.ppermute(sent, axis, [(i, i ^ step) for i in range(size)]))
+    blocks = jnp.stack(outs)[here ^ jnp.arange(size)]
+    return laid_out(blocks, concat_dim)
 
 
 def on_device(rhs_front, lower_blocks, panel_inverse, child_rows, child_map, child_owner):
@@ -55,7 +78,7 @@
         solution.reshape(held_blocks, block, width), row_at * share, share, 2
     )
     sending = jnp.einsum("dsk,kbr->dsbr", routing, mine, precision=highest)
-    received = lax.all_to_all(sending, "row", split_axis=0, concat_axis=3, tiled=True)
+    received = pairwise_exchange(sending, "row", 0, 3)
     return (solution, received.reshape(1, 1, most, block, width))
 
 

time: 1310 us -> 1310 us (level); the launches traced: 1300 us -> 1280 us
  blocking collectives: 85.4 us -> 0 us
  waiting for transfers between devices: 881 us -> 939 us
    all_to_all x1 -> x0, blocking collectives: 85.4 us -> none  [on_device(): lax.all_to_all(sending, 'row', split_axis=0, concat_axis=3, tiled=True)]
    ppermute x0 -> x3, waiting for transfers between devices: none -> 58.4 us  [pairwise_exchange(): outs.append(lax.ppermute(sent, axis, [(i, i ^ step) for i in range(size)]))]
  transfers between devices with their start and end apart: 8 -> 11, of which waited for: 8 -> 10; matrix products, arithmetic and copies ran while one was open for 2% -> 2% of each run, Pallas kernels for 0% -> 0%
where the time goes in v1:
time: 1310 us; the launch traced here: 1280 us
  waiting for transfers between devices  939 us (72%)
  matrix products  217 us (17%)
  local copies, waits for them, and re-layouts  91.6 us (7%)
  other arithmetic  15.6 us (1%)
  between operations  14.5 us (1%)
    psum x4, waiting for transfers between devices, on_device(): current = lax.psum(partial_value, 'row')  465 us
    psum x4, waiting for transfers between devices, on_device(): front = lax.psum(front, 'col')  416 us
    dot_general x6, matrix products, on_device(): jnp.dot(lower_blocks[panel * (panel - 1) // 2 + prior], solved[prior], pr...  116 us
    dot_general x4, matrix products, on_device(): jnp.dot(panel_inverse[panel], front, precision=highest, preferred_element...  78.1 us
    ppermute x3, waiting for transfers between devices, pairwise_exchange(): outs.append(lax.ppermute(sent, axis, [(i, i ^ step) for i in range(size)]))  58.4 us
    dot_general x1, local copies, waits for them, and re-layouts, on_device(): jnp.einsum('lk,kbr->lbr', picks, child_rows[0], precision=highest)  27.5 us
  transfers between devices with their start and end apart: 11, of which 10 were waited for; matrix products, arithmetic and copies ran while one was open for 2% of the time, Pallas kernels for 0%

profile of v1, /device:TPU:0, one launch (start us, length us, event | category | flops | bytes accessed | tf_op | source)
XLA Modules:
  0.0 1283.0 jit_solution(12286293096081295869)
XLA Ops:
  7.2 16.1 %fusion.38 = f32[48,128,1024]{2,0,1:T(8,128)S(1)} fusion(f32[8,128,1024]{2,1,0:T(8,128)} %bitcast.133, s32[8]{0:T(128)} %bitcast.141), kind=kOutput, calls=%fused_computation.42 | convolution fusion | flops 603980160 | bytes 29360160 | tf_op jit(solution)/shard_map/lk,kbr->lbr/dot_general | solution.py:46
  23.3 27.5 %copy.30 = f32[48,128,1024]{2,1,0:T(8,128)} copy(f32[48,128,1024]{2,0,1:T(8,128)S(1)} %fusion.38) | data formatting | bytes 50331648 | tf_op jit(solution)/shard_map/lk,kbr->lbr/dot_general | solution.py:46
  50.8 25.1 %copy.33 = f32[4,1536,1024]{1,2,0:T(8,128)} copy(f32[4,1536,1024]{2,1,0:T(8,128)} %bitcast.128) | data formatting | bytes 50331648 | tf_op jit(solution)/shard_map/reshape | solution.py:46
  78.3 4.1 add_dynamic-update-slice_fusion
  82.5 5.9 slice_bitcast_fusion.3
  88.5 106.8 %all-reduce.9.cloned.1.call-done = f32[1536,1024]{0,1:T(8,128)} async-done(((f32[1536,1024]{0,1:T(8,128)}), f32[1536,1024]{0,1:T(8,128)}) %all-reduce.9.cloned.1.call-update) | async-done | bytes 6291472 | tf_op jit(solution)/shard_map/psum | solution.py:70
  195.2 19.5 %fusion.45 = f32[768,1024]{0,1:T(8,128)} fusion(f32[1536,1024]{0,1:T(8,128)} %all-reduce.9.cloned.1.call-done, f32[4,768,1536]{2,1,0:T(8,128)} %param.8), kind=kOutput, calls=%fused_computation.48 | convolution fusion | flops 14495514624 | bytes 14155776 | tf_op jit(solution)/shard_map/dot_general | solution.py:71
  214.8 121.3 %all-reduce.11.cloned.1.call-done = f32[768,1024]{0,1:T(8,128)} async-done(((f32[768,1024]{0,1:T(8,128)}), f32[768,1024]{0,1:T(8,128)}) %all-reduce.11.cloned.1.call-update) | async-done | bytes 3145744 | tf_op jit(solution)/shard_map/psum | solution.py:74
  336.1 19.6 %fusion.5 = f32[1536,1024]{0,1:T(8,128)} fusion(f32[4,1536,1024]{1,2,0:T(8,128)} %add_dynamic-update-slice_fusion, f32[768,1024]{0,1:T(8,128)} %all-reduce.11.cloned.1.call-done, f32[6,1536,768]{2,1,0:T(8,128)} %param.7), kind=kOutput, calls=%fused_computation.10 | convolution fusion | flops 14497087488 | bytes 20447232 | tf_op jit(solution)/shard_map/dot_general | solution.py:64
  355.8 103.0 %all-reduce.13.cloned.1.call-done = f32[1536,1024]{0,1:T(8,128)} async-done(((f32[1536,1024]{0,1:T(8,128)}), f32[1536,1024]{0,1:T(8,128)}) %all-reduce.13.cloned.1.call-update) | async-done | bytes 6291472 | tf_op jit(solution)/shard_map/psum | solution.py:70
  458.8 19.6 %fusion.48 = f32[768,1024]{0,1:T(8,128)} fusion(f32[1536,1024]{0,1:T(8,128)} %all-reduce.13.cloned.1.call-done, f32[4,768,1536]{2,1,0:T(8,128)} %param.8), kind=kOutput, calls=%fused_computation.49 | convolution fusion | flops 14495514624 | bytes 14155776 | tf_op jit(solution)/shard_map/dot_general | solution.py:71
  478.5 121.2 %all-reduce.15.cloned.1.call-done = f32[768,1024]{0,1:T(8,128)} async-done(((f32[768,1024]{0,1:T(8,128)}), f32[768,1024]{0,1:T(8,128)}) %all-reduce.15.cloned.1.call-update) | async-done | bytes 3145744 | tf_op jit(solution)/shard_map/psum | solution.py:74
  599.8 18.3 %fusion.16 = f32[1024,1536]{1,0:T(8,128)S(1)} fusion(f32[768,1024]{0,1:T(8,128)} %all-reduce.15.cloned.1.call-done, f32[6,1536,768]{2,1,0:T(8,128)} %param.7), kind=kOutput, calls=%fused_computation.22 | convolution fusion | flops 14495514624 | bytes 14155776 | tf_op jit(solution)/shard_map/dot_general | solution.py:64
  618.0 19.5 %fusion.4 = f32[1536,1024]{0,1:T(8,128)} fusion(f32[4,1536,1024]{1,2,0:T(8,128)} %add_dynamic-update-slice_fusion, f32[1024,1536]{1,0:T(8,128)S(1)} %fusion.16, f32[768,1024]{0,1:T(8,128)S(1)} %copy-done, f32[6,1536,768]{2,1,0:T(8,128)} %param.7), kind=kOutput, calls=%fused_computation.8 | convolution fusion | flops 14498660352 | bytes 26738688 | tf_op jit(solution)/shard_map/dot_general | solution.py:64
  637.6 103.0 %all-reduce.17.cloned.1.call-done = f32[1536,1024]{0,1:T(8,128)} async-done(((f32[1536,1024]{0,1:T(8,128)}), f32[1536,1024]{0,1:T(8,128)}) %all-reduce.17.cloned.1.call-update) | async-done | bytes 6291472 | tf_op jit(solution)/shard_map/psum | solution.py:70
  740.7 19.5 %fusion.51 = f32[768,1024]{0,1:T(8,128)} fusion(f32[1536,1024]{0,1:T(8,128)} %all-reduce.17.cloned.1.call-done, f32[4,768,1536]{2,1,0:T(8,128)} %param.8), kind=kOutput, calls=%fused_computation.50 | convolution fusion | flops 14495514624 | bytes 14155776 | tf_op jit(solution)/shard_map/dot_general | solution.py:71
  760.2 20.0 %fusion.10 = f32[1024,1536]{1,0:T(8,128)} fusion(f32[768,1024]{0,1:T(8,128)} %all-reduce.15.cloned.1.call-done, f32[6,1536,768]{2,1,0:T(8,128)} %param.7), kind=kOutput, calls=%fused_computation.16 | convolution fusion | flops 14495514624 | bytes 14155776 | tf_op jit(solution)/shard_map/dot_general | solution.py:64
  780.2 101.3 %all-reduce.19.cloned.1.call-done = f32[768,1024]{0,1:T(8,128)} async-done(((f32[768,1024]{0,1:T(8,128)}), f32[768,1024]{0,1:T(8,128)}) %all-reduce.19.cloned.1.call-update) | async-done | bytes 3145744 | tf_op jit(solution)/shard_map/psum | solution.py:74
  881.5 19.2 %fusion.8 = f32[1024,1536]{1,0:T(8,128)S(1)} fusion(f32[768,1024]{0,1:T(8,128)} %all-reduce.19.cloned.1.call-done, f32[6,1536,768]{2,1,0:T(8,128)} %param.7), kind=kOutput, calls=%fused_computation.14 | convolution fusion | flops 14495514624 | bytes 14155776 | tf_op jit(solution)/shard_map/dot_general | solution.py:64
  900.7 19.9 %fusion.2 = f32[1536,1024]{0,1:T(8,128)} fusion(f32[4,1536,1024]{1,2,0:T(8,128)} %add_dynamic-update-slice_fusion, f32[1024,1536]{1,0:T(8,128)S(1)} %fusion.8, f32[1024,1536]{1,0:T(8,128)S(1)} %copy-done.1, f32[768,1024]{0,1:T(8,128)S(1)} %copy-done, f32[6,1536,768]{2,1,0:T(8,128)} %param.7), kind=kOutput, calls=%fused_computation.5 | convolution fusion | flops 14500233216 | bytes 33030144 | tf_op jit(solution)/shard_map/dot_general | solution.py:64
  920.6 103.0 %all-reduce.21.cloned.1.call-done = f32[1536,1024]{0,1:T(8,128)} async-done(((f32[1536,1024]{0,1:T(8,128)}), f32[1536,1024]{0,1:T(8,128)}) %all-reduce.21.cloned.1.call-update) | async-done | bytes 6291472 | tf_op jit(solution)/shard_map/psum | solution.py:70
  1023.6 19.5 %fusion.54 = f32[1,768,1024]{1,2,0:T(8,128)} fusion(f32[1536,1024]{0,1:T(8,128)} %all-reduce.21.cloned.1.call-done, f32[4,768,1536]{2,1,0:T(8,128)} %param.8), kind=kOutput, calls=%fused_computation.51 | convolution fusion | flops 14495514624 | bytes 14155776 | tf_op jit(solution)/shard_map/dot_general | solution.py:71
  1043.4 121.1 %all-reduce.23.cloned.1.call-done = f32[1,768,1024]{1,2,0:T(8,128)} async-done(((f32[1,768,1024]{1,2,0:T(8,128)}), f32[1,768,1024]{1,2,0:T(8,128)}) %all-reduce.23.cloned.1.call-update) | async-done | bytes 3145744 | tf_op jit(solution)/shard_map/psum | solution.py:74
  1164.5 9.1 pad_maximum_fusion
  1173.6 12.8 copy.42
  1188.6 6.5 fusion.44
  1198.1 2.8 collective-permute-start.2
  1201.2 35.3 %collective-permute-done = f32[1,7,128,256]{3,2,1,0:T(8,128)S(1)} collective-permute-done((f32[1,7,128,256]{3,2,1,0:T(8,128)S(1)}, f32[1,7,128,256]{3,2,1,0:T(8,128)S(1)}, u32[]{:S(2)}, u32[]{:S(2)}) %collective-permute-start) | collective-permute-done | bytes 917536 | tf_op jit(solution)/shard_map/ppermute | solution.py:25
  1236.6 23.1 %collective-permute-done.1 = f32[1,7,128,256]{3,2,1,0:T(8,128)S(1)} collective-permute-done((f32[1,7,128,256]{3,2,1,0:T(8,128)S(1)}, f32[1,7,128,256]{3,2,1,0:T(8,128)S(1)}, u32[]{:S(2)}, u32[]{:S(2)}) %collective-permute-start.1) | collective-permute-done | bytes 917536 | tf_op jit(solution)/shard_map/ppermute | solution.py:25
  1261.7 4.6 gather_fusion
  1266.3 4.6 copy.41
  1270.9 5.0 copy.43
  (38 shorter events, 10.6 us)
Async XLA Ops:
  7.2 188.1 %all-reduce.9.cloned.1.call-start = ((), (), s32[]{:S(2)}) async-start(), calls=%async_computation | async-start | bytes 12582912 | tf_op jit(solution)/shard_map/psum | solution.py:70
  88.4 247.6 %all-reduce.11.cloned.1.call-start = ((), (), s32[]{:S(2)}) async-start(), calls=%async_computation.1 | async-start | bytes 6291456 | tf_op jit(solution)/shard_map/psum | solution.py:74
  214.8 244.0 %all-reduce.13.cloned.1.call-start = ((), (), s32[]{:S(2)}) async-start(), calls=%async_computation.2 | async-start | bytes 12582912 | tf_op jit(solution)/shard_map/psum | solution.py:70
  355.7 244.0 %all-reduce.15.cloned.1.call-start = ((), (), s32[]{:S(2)}) async-start(), calls=%async_computation.3 | async-start | bytes 6291456 | tf_op jit(solution)/shard_map/psum | solution.py:74
  478.4 139.6 %copy-start = (f32[768,1024]{0,1:T(8,128)S(1)}, f32[768,1024]{0,1:T(8,128)}, u32[]{:S(2)}) copy-start(f32[768,1024]{0,1:T(8,128)} %all-reduce.11.cloned.1.call-done) | copy-start | bytes 9437188
  478.5 262.2 %all-reduce.17.cloned.1.call-start = ((), (), s32[]{:S(2)}) async-start(), calls=%async_computation.4 | async-start | bytes 12582912 | tf_op jit(solution)/shard_map/psum | solution.py:70
  637.6 243.9 %all-reduce.19.cloned.1.call-start = ((), (), s32[]{:S(2)}) async-start(), calls=%async_computation.5 | async-start | bytes 6291456 | tf_op jit(solution)/shard_map/psum | solution.py:74
  760.2 263.5 %all-reduce.21.cloned.1.call-start = ((), (), s32[]{:S(2)}) async-start(), calls=%async_computation.6 | async-start | bytes 12582912 | tf_op jit(solution)/shard_map/psum | solution.py:70
  881.5 19.2 %copy-start.1 = (f32[1024,1536]{1,0:T(8,128)S(1)}, f32[1024,1536]{1,0:T(8,128)}, u32[]{:S(2)}) copy-start(f32[1024,1536]{1,0:T(8,128)} %fusion.10) | copy-start | bytes 18874372
  920.6 122.6 %copy-start.2 = (s32[1,24,1]{1,2,0:T(1,128)S(1)}, s32[1,24,1]{1,2,0:T(1,128)}, u32[]{:S(2)}) copy-start(s32[1,24,1]{1,2,0:T(1,128)} %param.11) | copy-start | bytes 292
  920.6 243.9 %all-reduce.23.cloned.1.call-start = ((), (), s32[]{:S(2)}) async-start(), calls=%async_computation.7 | async-start | bytes 6291456 | tf_op jit(solution)/shard_map/psum | solution.py:74
  1195.7 40.8 %collective-permute-start = (f32[1,7,128,256]{3,2,1,0:T(8,128)S(1)}, f32[1,7,128,256]{3,2,1,0:T(8,128)S(1)}, u32[]{:S(2)}, u32[]{:S(2)}) collective-permute-start(f32[1,7,128,256]{3,2,1,0:T(8,128)S(1)} %copy.37), channel_id=1, source_target_pairs={{0,8},{8,0},{16,24},{24,16},{1,9},{9,1},{17,25},{25,17},{2,10},{10... | collective-permute-start | bytes 2752520 | tf_op jit(solution)/shard_map/ppermute | solution.py:25
  1196.1 63.5 %collective-permute-start.1 = (f32[1,7,128,256]{3,2,1,0:T(8,128)S(1)}, f32[1,7,128,256]{3,2,1,0:T(8,128)S(1)}, u32[]{:S(2)}, u32[]{:S(2)}) collective-permute-start(f32[1,7,128,256]{3,2,1,0:T(8,128)S(1)} %copy.38), channel_id=1, source_target_pairs={{0,16},{8,24},{16,0},{24,8},{1,17},{9,25},{17,1},{25,9},{2,18},{10... | collective-permute-start | bytes 2752520 | tf_op jit(solution)/shard_map/ppermute | solution.py:25
  1198.1 61.5 %collective-permute-start.2 = (f32[1,7,128,256]{3,2,1,0:T(8,128)S(1)}, f32[1,7,128,256]{3,2,1,0:T(8,128)S(1)}, u32[]{:S(2)}, u32[]{:S(2)}) collective-permute-start(f32[1,7,128,256]{3,2,1,0:T(8,128)S(1)} %copy.39), channel_id=1, source_target_pairs={{0,24},{8,16},{16,8},{24,0},{1,25},{9,17},{17,9},{25,1},{2,26},{10... | collective-permute-start | bytes 2752520 | tf_op jit(solution)/shard_map/ppermute | solution.py:25
Sparse Core Ops, SparseCore 0:
  88.6 106.6 all-reduce.8
  214.9 121.1 all-reduce.10
  355.8 102.8 all-reduce.12
  478.6 121.1 all-reduce.14
  637.7 102.9 all-reduce.16
  760.3 121.1 all-reduce.18
  920.7 102.9 all-reduce.20
  1043.3 121.1 all-reduce.22
